TPU v7x, 32 devices: a whole 2x2x4 slice. The times are simulated.
32 devices in a mesh: band: 4 (over x, core), grid: 8 (over z, y).
Axes of the slice: x: 2, y: 2, z: 4, core: 2. Of those that a mesh axis runs over, the one named last changes fastest.
Arguments:
- states: float32 [64, 64, 8, 128], P('band', 'grid'), may hold values from -6 to 6
- potential: float32 [64, 8, 128], P('grid'), may hold values from -1 to 1
- proj_index: int32 [16, 128], replicated, may hold values from 0 to 65535, as said below
- proj_value: float32 [16, 128], replicated, may hold values from 0 to 1
- proj_strength: float32 [16], replicated, may hold values from 0.5 to 4
Outputs:
- filtered: float32 [64, 64, 8, 128], P('band', 'grid')
- gram: float32 [64, 64], P('band')
- hamiltonian: float32 [64, 64], P('band')
Inputs may be any that keep to these rules, and one draw needn't show every extreme that they name: `proj_index`: along the first grid dimension every support point lies within 8 planes of its atom's centre plane.
All inputs are finite; a program needn't handle non-finite values.
Results may differ from a plain program's by a relative error of at most 0.0001.
Values sent between devices are 32-bit elements; how exact they have to be, the bound alone decides.
A program may use at most 64 MiB of HBM per device.

v0:
```python
import jax
import jax.numpy as jnp
from jax import lax
from jax.sharding import PartitionSpec as P

RADIUS = 4
DEGREE = 4


stencil_weights = (-205.0 / 72.0, 1.6, -0.2, 8.0 / 315.0, -1.0 / 560.0)
filter_centre = 10.0
filter_half = 6.0


def padded_2(block, sides, width):
    for axis, dim in sides:
        count = lax.axis_size(axis)
        forward = [(i, i + 1) for i in range(count - 1)]
        backward = [(target, source) for source, target in forward]
        low = lax.ppermute(
            lax.slice_in_dim(block, block.shape[dim] - width, None, axis=dim), axis, forward
        )
        high = lax.ppermute(lax.slice_in_dim(block, 0, width, axis=dim), axis, backward)
        block = jnp.concatenate([low, block, high], axis=dim)
    return block


def kinetic(padded):
    extent = padded.shape[-3] - 2 * RADIUS
    middle = padded[..., RADIUS : RADIUS + extent, :, :]
    grid_rows = middle.shape[-2]
    grid_cols = middle.shape[-1]
    pad_widths = [(0, 0)] * (middle.ndim - 2) + [(RADIUS, RADIUS), (RADIUS, RADIUS)]
    padded_yz = jnp.pad(middle, pad_widths)
    summed = 3.0 * stencil_weights[0] * middle
    for shift_by in range(1, RADIUS + 1):
        neighbours = (
            padded[..., RADIUS + shift_by : RADIUS + shift_by + extent, :, :]
            + padded[..., RADIUS - shift_by : RADIUS - shift_by + extent, :, :]
        )
        neighbours = (
            neighbours
            + padded_yz[
                ..., RADIUS + shift_by : RADIUS + shift_by + grid_rows, RADIUS : RADIUS + grid_cols
            ]
            + padded_yz[
                ..., RADIUS - shift_by : RADIUS - shift_by + grid_rows, RADIUS : RADIUS + grid_cols
            ]
        )
        neighbours = (
            neighbours
            + padded_yz[
                ..., RADIUS : RADIUS + grid_rows, RADIUS + shift_by : RADIUS + shift_by + grid_cols
            ]
            + padded_yz[
                ..., RADIUS : RADIUS + grid_rows, RADIUS - shift_by : RADIUS - shift_by + grid_cols
            ]
        )
        summed = summed + stencil_weights[shift_by] * neighbours
    return -0.5 * summed


def inner_rows(left, right):
    return lax.dot_general(
        left,
        right,
        (((1,), (1,)), ((), ())),
        precision=lax.Precision.HIGHEST,
        preferred_element_type=jnp.float32,
    )


def per_device(states, potential, proj_index, proj_value, proj_strength):
    state_count, planes, grid_rows, grid_cols = states.shape
    points = planes * grid_rows * grid_cols
    atom_count = proj_index.shape[0]
    offset = lax.axis_index("grid") * points
    local_idx = proj_index - offset
    inside = (local_idx >= 0) & (local_idx < points)
    safe_idx = jnp.where(inside, local_idx, 0)
    weights = jnp.where(inside, proj_value, 0.0)
    atom_rows = jnp.broadcast_to(jnp.arange(atom_count, dtype=jnp.int32)[:, None], safe_idx.shape)
    projector = jnp.zeros((atom_count, points), jnp.float32).at[atom_rows, safe_idx].add(weights)

    def apply_h(field):
        padded = padded_2(field, (("grid", 1),), RADIUS)
        kinetic_v = kinetic(padded)
        flat_v = field.reshape(state_count, points)
        partial_value = inner_rows(flat_v, projector)
        coeffs = lax.psum(partial_value, "grid")
        scaled = coeffs * proj_strength[None, :]
        nonlocal_v = jnp.dot(
            scaled, projector, precision=lax.Precision.HIGHEST, preferred_element_type=jnp.float32
        )
        return kinetic_v + potential * field + nonlocal_v.reshape(field.shape)

    previous = states
    current = (apply_h(states) - filter_centre * states) / filter_half
    for degree_k in range(1, DEGREE):
        following = 2.0 * (apply_h(current) - filter_centre * current) / filter_half - previous
        previous = current
        current = following
    images = apply_h(current)
    flat_y = current.reshape(state_count, points)
    flat_h = images.reshape(state_count, points)
    total_points = float(points * lax.axis_size("grid"))
    gathered = lax.all_gather(flat_y, "band", axis=0, tiled=True)
    partial_blocks = jnp.stack([inner_rows(flat_y, gathered), inner_rows(flat_h, gathered)])
    blocks = lax.psum(partial_blocks, "grid")
    gram = blocks[0] / total_points
    hamiltonian = blocks[1] / total_points
    return (current, gram, hamiltonian)


def solution(mesh):
    in_specs = (P("band", "grid", None, None), P("grid", None, None), P(), P(), P())
    out_specs = (P("band", "grid", None, None), P("band", None), P("band", None))
    return jax.shard_map(
        per_device, mesh=mesh, in_specs=in_specs, out_specs=out_specs, check_vma=False
    )
```

profile of v0, /device:TPU:0, one launch (start us, length us, event | category | flops | bytes accessed | tf_op | source)
XLA Modules:
  0.0 211.4 jit_solution(2648983875373184538)
XLA Ops:
  7.2 0.0 copy-start.1
  7.2 0.0 all-gather.2.cloned.1.call-start
  7.2 1.1 fusion.219
  8.4 4.9 %collective-permute-start.1 = (f32[16,4,8,128]{3,2,1,0:T(8,128)S(1)}, f32[16,4,8,128]{3,2,1,0:T(8,128)S(1)}, u32[]{:S(2)}, u32[]{:S(2)}) collective-permute-start(f32[16,4,8,128]{3,2,1,0:T(8,128)S(1)} %get-tuple-element.14), channel_id=1, source_target_pairs={{0,1},{1,2},{2,3},{3,4},{4,5},{5,6},{6,7},{8,9},{9,10},{10,11},{11... | collective-permute-start | bytes 786440 | tf_op jit(solution)/shard_map/ppermute | solution.py:20
  13.3 1.3 collective-permute-start
  14.6 0.7 fusion.200
  15.3 0.7 and_reduce_fusion
  16.0 0.7 multiply_reduce_fusion
  16.8 0.7 select_bitcast_fusion.1
  17.5 14.4 %scatter_custom_fusion = f32[131072]{0:T(1024)S(1)} fusion(s32[2048]{0:T(1024)S(1)} %select_bitcast_fusion, f32[2048]{0:T(1024)S(1)} %select_bitcast_fusion.1, f32[]{:T(128)} %constant.17.clone.1), kind=kCustom, calls=%fused_computation.348 | custom fusion | flops 2048 | bytes 524292
  31.8 0.1 reshape.72
  32.0 0.9 convolution_bitcast_fusion.5
  32.9 22.9 %psum.42 = f32[16,16]{0,1:T(8,128)S(1)} all-reduce(f32[16,16]{0,1:T(8,128)S(1)} %convolution_bitcast_fusion.5), channel_id=1, replica_groups=mesh['band'=4,'grid'=8] {'grid'}, use_global_device_ids=true, to_apply=%region_1.2 | all-reduce | flops 256 | bytes 2048 | tf_op jit(solution)/shard_map/psum | solution.py:90
  55.8 0.7 convolution_bitcast_fusion.4
  56.5 0.1 copy.9
  56.6 0.0 collective-permute-done.1
  56.7 0.1 constant_dynamic-update-slice_fusion.1
  56.8 0.0 collective-permute-done
  56.8 1.2 broadcast_multiply_fusion
  58.0 0.7 fusion.218
  58.7 1.3 collective-permute-start.3
  60.0 1.3 collective-permute-start.2
  61.3 1.0 fusion.189
  62.3 20.5 %psum.43 = f32[16,16]{0,1:T(8,128)S(1)} all-reduce(f32[16,16]{0,1:T(8,128)S(1)} %fusion.189), channel_id=1, replica_groups=mesh['band'=4,'grid'=8] {'grid'}, use_global_device_ids=true, to_apply=%region_2.3 | all-reduce | flops 256 | bytes 2048 | tf_op jit(solution)/shard_map/psum | solution.py:90
  82.8 0.7 convolution_bitcast_fusion.3
  83.5 0.1 copy.11
  83.6 0.0 collective-permute-done.3
  83.6 0.0 collective-permute-done.2
  83.6 1.3 fusion.113
  85.0 1.3 collective-permute-start.5
  86.3 1.3 collective-permute-start.4
  87.6 1.0 fusion.186
  88.6 20.3 %psum.44 = f32[16,16]{0,1:T(8,128)S(1)} all-reduce(f32[16,16]{0,1:T(8,128)S(1)} %fusion.186), channel_id=1, replica_groups=mesh['band'=4,'grid'=8] {'grid'}, use_global_device_ids=true, to_apply=%region_3.4 | all-reduce | flops 256 | bytes 2048 | tf_op jit(solution)/shard_map/psum | solution.py:90
  109.0 0.7 convolution_bitcast_fusion.2
  109.7 0.1 copy.13
  109.8 0.0 collective-permute-done.5
  109.8 0.0 collective-permute-done.4
  109.8 1.3 fusion.79
  111.1 1.8 collective-permute-start.7
  112.9 1.3 collective-permute-start.6
  114.2 1.0 fusion.183
  115.2 20.2 %psum.45 = f32[16,16]{0,1:T(8,128)S(1)} all-reduce(f32[16,16]{0,1:T(8,128)S(1)} %fusion.183), channel_id=1, replica_groups=mesh['band'=4,'grid'=8] {'grid'}, use_global_device_ids=true, to_apply=%region_4.5 | all-reduce | flops 256 | bytes 2048 | tf_op jit(solution)/shard_map/psum | solution.py:90
  135.4 0.7 convolution_bitcast_fusion.1
  136.1 0.1 copy.15
  136.2 0.0 collective-permute-done.7
  136.2 0.0 collective-permute-done.6
  136.2 1.3 fusion.45
  137.5 0.0 copy-start
  137.5 1.1 copy.42
  138.6 0.0 all-gather.2.cloned.1.call-update
  138.7 1.5 collective-permute-start.9
  140.2 1.3 collective-permute-start.8
  141.5 1.0 fusion.213
  142.5 20.9 %psum.46 = f32[16,16]{0,1:T(8,128)S(1)} all-reduce(f32[16,16]{0,1:T(8,128)S(1)} %fusion.213), channel_id=1, replica_groups=mesh['band'=4,'grid'=8] {'grid'}, use_global_device_ids=true, to_apply=%region_5.6 | all-reduce | flops 256 | bytes 2048 | tf_op jit(solution)/shard_map/psum | solution.py:90
  163.5 0.7 convolution_bitcast_fusion
  164.2 0.1 copy.17
  164.3 0.0 collective-permute-done.9
  164.3 0.0 collective-permute-done.8
  164.3 1.3 fusion.11
  165.6 0.0 all-gather.2.cloned.1.call-done
  165.6 3.5 %convolution_bitcast_fusion.7 = f32[1,16,64]{2,1,0:T(8,128)S(1)} fusion(f32[64,8192]{1,0:T(8,128)} %all-gather.2.cloned.1.call-done, f32[2,8,64,128]{3,2,1,0:T(8,128)S(1)} %bitcast.82), kind=kOutput, calls=%fused_computation.112 | convolution fusion | flops 100663296 | bytes 2625536 | tf_op jit(solution)/shard_map/dot_general | solution.py:64
  169.1 1.7 convolution_bitcast_fusion.6
  170.8 33.1 %psum.47 = f32[2,16,64]{2,1,0:T(8,128)S(1)} all-reduce(f32[2,16,64]{2,1,0:T(8,128)S(1)} %pad_maximum_fusion.8), channel_id=1, replica_groups=mesh['band'=4,'grid'=8] {'grid'}, use_global_device_ids=true, to_apply=%region_6.7 | all-reduce | flops 2048 | bytes 16384 | tf_op jit(solution)/shard_map/psum | solution.py:109
  203.9 0.6 fusion.201
  (17 shorter events, 0.2 us)
Async XLA Ops:
  7.2 24.8 %copy-start.1 = (f32[16,8,8,128]{3,2,1,0:T(8,128)S(1)}, f32[16,8,8,128]{3,2,1,0:T(8,128)}, u32[]{:S(2)}) copy-start(f32[16,8,8,128]{3,2,1,0:T(8,128)} %param.5) | copy-start | bytes 1572868
  7.2 48.6 %copy-start.3 = (f32[8,8,128]{2,1,0:T(8,128)S(1)}, f32[8,8,128]{2,1,0:T(8,128)}, u32[]{:S(2)}) copy-start(f32[8,8,128]{2,1,0:T(8,128)} %param.6) | copy-start | bytes 98308
  7.2 48.6 %copy-start.4 = (f32[16]{0:T(128)S(1)}, f32[16]{0:T(128)}, u32[]{:S(2)}) copy-start(f32[16]{0:T(128)} %param.9) | copy-start | bytes 196
  7.2 158.4 %all-gather.2.cloned.1.call-start = ((), (), s32[]{:S(2)}) async-start(), calls=%async_computation | async-start | bytes 2621440 | tf_op jit(solution)/shard_map/all_gather | solution.py:107
  8.4 48.3 %collective-permute-start.1 = (f32[16,4,8,128]{3,2,1,0:T(8,128)S(1)}, f32[16,4,8,128]{3,2,1,0:T(8,128)S(1)}, u32[]{:S(2)}, u32[]{:S(2)}) collective-permute-start(f32[16,4,8,128]{3,2,1,0:T(8,128)S(1)} %get-tuple-element.14), channel_id=1, source_target_pairs={{0,1},{1,2},{2,3},{3,4},{4,5},{5,6},{6,7},{8,9},{9,10},{10,11},{11... | collective-permute-start | bytes 786440 | tf_op jit(solution)/shard_map/ppermute | solution.py:20
  13.3 43.5 %collective-permute-start = (f32[16,4,8,128]{3,2,1,0:T(8,128)S(1)}, f32[16,4,8,128]{3,2,1,0:T(8,128)S(1)}, u32[]{:S(2)}, u32[]{:S(2)}) collective-permute-start(f32[16,4,8,128]{3,2,1,0:T(8,128)S(1)} %get-tuple-element.13), channel_id=1, source_target_pairs={{1,0},{2,1},{3,2},{4,3},{5,4},{6,5},{7,6},{9,8},{10,9},{11,10},{12... | collective-permute-start | bytes 786440 | tf_op jit(solution)/shard_map/ppermute | solution.py:23
  58.7 24.9 %collective-permute-start.3 = (f32[16,4,8,128]{3,2,1,0:T(8,128)}, f32[16,4,8,128]{3,2,1,0:T(8,128)S(1)}, u32[]{:S(2)}, u32[]{:S(2)}) collective-permute-start(f32[16,4,8,128]{3,2,1,0:T(8,128)} %get-tuple-element.12), channel_id=1, source_target_pairs={{0,1},{1,2},{2,3},{3,4},{4,5},{5,6},{6,7},{8,9},{9,10},{10,11},{11... | collective-permute-start | bytes 786440 | tf_op jit(solution)/shard_map/ppermute | solution.py:20
  60.0 23.6 %collective-permute-start.2 = (f32[16,4,8,128]{3,2,1,0:T(8,128)S(1)}, f32[16,4,8,128]{3,2,1,0:T(8,128)S(1)}, u32[]{:S(2)}, u32[]{:S(2)}) collective-permute-start(f32[16,4,8,128]{3,2,1,0:T(8,128)S(1)} %get-tuple-element.11), channel_id=1, source_target_pairs={{1,0},{2,1},{3,2},{4,3},{5,4},{6,5},{7,6},{9,8},{10,9},{11,10},{12... | collective-permute-start | bytes 786440 | tf_op jit(solution)/shard_map/ppermute | solution.py:23
  85.0 24.8 %collective-permute-start.5 = (f32[16,4,8,128]{3,2,1,0:T(8,128)S(1)}, f32[16,4,8,128]{3,2,1,0:T(8,128)S(1)}, u32[]{:S(2)}, u32[]{:S(2)}) collective-permute-start(f32[16,4,8,128]{3,2,1,0:T(8,128)S(1)} %get-tuple-element.10), channel_id=1, source_target_pairs={{0,1},{1,2},{2,3},{3,4},{4,5},{5,6},{6,7},{8,9},{9,10},{10,11},{11... | collective-permute-start | bytes 786440 | tf_op jit(solution)/shard_map/ppermute | solution.py:20
  86.3 23.5 %collective-permute-start.4 = (f32[16,4,8,128]{3,2,1,0:T(8,128)S(1)}, f32[16,4,8,128]{3,2,1,0:T(8,128)S(1)}, u32[]{:S(2)}, u32[]{:S(2)}) collective-permute-start(f32[16,4,8,128]{3,2,1,0:T(8,128)S(1)} %get-tuple-element.9), channel_id=1, source_target_pairs={{1,0},{2,1},{3,2},{4,3},{5,4},{6,5},{7,6},{9,8},{10,9},{11,10},{12... | collective-permute-start | bytes 786440 | tf_op jit(solution)/shard_map/ppermute | solution.py:23
  111.1 25.1 %collective-permute-start.7 = (f32[16,4,8,128]{3,2,1,0:T(8,128)S(1)}, f32[16,4,8,128]{3,2,1,0:T(8,128)S(1)}, u32[]{:S(2)}, u32[]{:S(2)}) collective-permute-start(f32[16,4,8,128]{3,2,1,0:T(8,128)S(1)} %get-tuple-element.8), channel_id=1, source_target_pairs={{0,1},{1,2},{2,3},{3,4},{4,5},{5,6},{6,7},{8,9},{9,10},{10,11},{11... | collective-permute-start | bytes 786440 | tf_op jit(solution)/shard_map/ppermute | solution.py:20
  112.9 23.3 %collective-permute-start.6 = (f32[16,4,8,128]{3,2,1,0:T(8,128)S(1)}, f32[16,4,8,128]{3,2,1,0:T(8,128)S(1)}, u32[]{:S(2)}, u32[]{:S(2)}) collective-permute-start(f32[16,4,8,128]{3,2,1,0:T(8,128)S(1)} %get-tuple-element.7), channel_id=1, source_target_pairs={{1,0},{2,1},{3,2},{4,3},{5,4},{6,5},{7,6},{9,8},{10,9},{11,10},{12... | collective-permute-start | bytes 786440 | tf_op jit(solution)/shard_map/ppermute | solution.py:23
  137.5 28.1 %copy-start = (f32[16,8,8,128]{3,2,1,0:T(8,128)}, f32[16,8,8,128]{3,2,1,0:T(8,128)S(1)}, u32[]{:S(2)}) copy-start(f32[16,8,8,128]{3,2,1,0:T(8,128)S(1)} %fusion.45) | copy-start | bytes 1572868
  138.7 25.6 %collective-permute-start.9 = (f32[16,4,8,128]{3,2,1,0:T(8,128)S(1)}, f32[16,4,8,128]{3,2,1,0:T(8,128)S(1)}, u32[]{:S(2)}, u32[]{:S(2)}) collective-permute-start(f32[16,4,8,128]{3,2,1,0:T(8,128)S(1)} %get-tuple-element.6), channel_id=1, source_target_pairs={{0,1},{1,2},{2,3},{3,4},{4,5},{5,6},{6,7},{8,9},{9,10},{10,11},{11... | collective-permute-start | bytes 786440 | tf_op jit(solution)/shard_map/ppermute | solution.py:20
  140.2 24.1 %collective-permute-start.8 = (f32[16,4,8,128]{3,2,1,0:T(8,128)S(1)}, f32[16,4,8,128]{3,2,1,0:T(8,128)S(1)}, u32[]{:S(2)}, u32[]{:S(2)}) collective-permute-start(f32[16,4,8,128]{3,2,1,0:T(8,128)S(1)} %get-tuple-element.5), channel_id=1, source_target_pairs={{1,0},{2,1},{3,2},{4,3},{5,4},{6,5},{7,6},{9,8},{10,9},{11,10},{12... | collective-permute-start | bytes 786440 | tf_op jit(solution)/shard_map/ppermute | solution.py:23
  165.6 3.5 %copy-start.2 = (f32[64,8192]{1,0:T(8,128)S(1)}, f32[64,8192]{1,0:T(8,128)}, u32[]{:S(2)}) copy-start(f32[64,8192]{1,0:T(8,128)} %all-gather.2.cloned.1.call-done) | copy-start | bytes 6291460
Sparse Core Ops, SparseCore 0:
  138.8 20.2 all-gather.1
where the time goes:
time: 212 us; the launch traced here: 211 us
  blocking collectives  138 us (65%)
  other arithmetic  24.2 us (11%)
  starting transfers between devices  17.3 us (8%)
  between operations  14.5 us (7%)
  matrix products  13.6 us (6%)
  local copies, waits for them, and re-layouts  3.87 us (2%)
    psum x5, blocking collectives, apply_h(): coeffs = lax.psum(partial_value, 'grid')  105 us
    psum x1, blocking collectives, per_device(): blocks = lax.psum(partial_blocks, 'grid')  33.1 us
    unnamed x4, other arithmetic  15.8 us
    ppermute x5, starting transfers between devices, padded_2(): lax.ppermute(lax.slice_in_dim(block, block.shape[dim] - width, None, axis...  10.8 us
    dot_general x7, matrix products, inner_rows(): lax.dot_general(left, right, (((1,), (1,)), ((), ())), precision=lax.Prec...  10.1 us
    ppermute x5, starting transfers between devices, padded_2(): lax.ppermute(lax.slice_in_dim(block, 0, width, axis=dim), axis, backward)  6.46 us
  transfers between devices with their start and end apart: 11, of which 0 were waited for; matrix products, arithmetic and copies ran while one was open for 13% of the time, Pallas kernels for 0%

commit v1 on v0

v1 whole, which is shorter than its diff:
```python
import functools

import jax
import jax.numpy as jnp
from jax import lax
from jax.experimental import pallas as pl
from jax.experimental.pallas import tpu as pltpu
from jax.sharding import PartitionSpec as P

RADIUS = 4
DEGREE = 4
LANES = 128
MESH = pl.DeviceIdType.MESH

stencil_weights = (-205.0 / 72.0, 1.6, -0.2, 8.0 / 315.0, -1.0 / 560.0)
filter_centre = 10.0
filter_half = 6.0


def kernel(
    bands, slabs, planes, rows, cols, atoms, total_points,
    states, potential, index_ref, value_ref, strength_ref,
    out_ref, gram_ref, ham_ref,
    field, image, pot, proj, coef_mine, coef_far, coef_wide, slab_y, both, prod, band_sum, mine, grid_sum,
    send, recv, local,
):
    half = states.shape[0] // 2
    area = rows * cols
    chunk = 2 * planes
    me_b, me_g = lax.axis_index("band"), lax.axis_index("grid")
    pair, side = me_g // 2, me_g % 2
    other = 1 - side
    last_pair = slabs // 2 - 1
    has_down, has_up = pair > 0, pair < last_pair
    counter = [0]

    def remote(src, dst, slot, where):
        return pltpu.make_async_remote_copy(
            src_ref=src, dst_ref=dst, send_sem=send.at[slot], recv_sem=recv.at[slot],
            device_id=where, device_id_type=MESH,
        )

    def slots(count):
        first = counter[0]
        counter[0] += count
        return first

    def lanes(start, count):
        return pl.ds(pl.multiple_of(start, LANES), count)

    for k in range(DEGREE + 1):
        field[k, :, 0 : RADIUS * area] = jnp.zeros((half, RADIUS * area), jnp.float32)
        field[k, :, (RADIUS + chunk) * area :] = jnp.zeros((half, RADIUS * area), jnp.float32)
    coef_far[...] = jnp.zeros_like(coef_far)

    barrier = pltpu.get_barrier_semaphore()
    peers = [(me_b, lax.rem(me_g + d, slabs)) for d in range(1, slabs)]
    crossing = [
        (lax.rem(me_b + d, bands), 2 * pair + lax.rem(side + e, 2)) for d in range(1, bands) for e in range(2)
    ]
    for peer in peers + crossing:
        pl.semaphore_signal(barrier, inc=1, device_id=peer, device_id_type=MESH)
    pl.semaphore_wait(barrier, len(peers) + len(crossing))

    partner = (me_b, 2 * pair + other)
    up, down = (me_b, me_g + 2), (me_b, me_g - 2)

    here = lanes((RADIUS + side * planes) * area, planes * area)
    first = slots(2)
    swaps = [
        remote(potential, pot.at[pl.ds(side * planes, planes)], first, partner),
        remote(states.at[pl.ds(pl.multiple_of(other * half, half), half)], field.at[0, :, here], first + 1, partner),
    ]
    for copy in swaps:
        copy.start()
    own = [
        pltpu.make_async_copy(potential, pot.at[pl.ds(side * planes, planes)], local.at[0]),
        pltpu.make_async_copy(
            states.at[pl.ds(pl.multiple_of(side * half, half), half)], field.at[0, :, here], local.at[1]
        ),
    ]
    for copy in own:
        copy.start()

    points = index_ref.shape[1]
    row_iota = lax.broadcasted_iota(jnp.int32, (chunk * rows, points), 0) + pair * (chunk * rows)
    col_iota = lax.broadcasted_iota(jnp.int32, (cols, points), 0)

    def build(a, carry):
        idx = index_ref[pl.ds(a, 1), :]
        row = lax.div(idx, cols)
        col = idx - row * cols
        left = jnp.where(row_iota == row, value_ref[pl.ds(a, 1), :], 0.0)
        right = jnp.where(col_iota == col, 1.0, 0.0)
        proj[a] = lax.dot_general(
            left, right, (((1,), (1,)), ((), ())),
            precision=lax.Precision.HIGHEST, preferred_element_type=jnp.float32,
        )
        return carry

    lax.fori_loop(0, atoms, build, 0)

    col = lax.broadcasted_iota(jnp.int32, (half, cols), 1)
    wide = coef_mine.shape[-1]
    wide_iota = lax.broadcasted_iota(jnp.int32, (half, wide), 1)
    block = 8

    def plane_at(src, p):
        return src[:, lanes((p + RADIUS) * area, area)]

    def project(k):
        def atoms_of(j, tile):
            def at_plane(p, sums):
                v = plane_at(field.at[k], p)
                parts = []
                for i in range(block):
                    s = sums[i]
                    for y in range(rows):
                        s = s + v[:, y * cols : (y + 1) * cols] * proj[j * block + i, pl.ds(p * rows + y, 1), :]
                    parts.append(s)
                return tuple(parts)

            sums = lax.fori_loop(0, chunk, at_plane, tuple(jnp.zeros((half, cols), jnp.float32) for _ in range(block)))
            for i in range(block):
                tile = jnp.where(wide_iota == j * block + i, jnp.sum(sums[i], axis=1, keepdims=True), tile)
            return tile

        return lax.fori_loop(0, atoms // block, atoms_of, jnp.zeros((half, wide), jnp.float32))

    def local_part(src, p, a, b):
        c = plane_at(src, p)
        cell = [c[:, y * cols : (y + 1) * cols] for y in range(rows)]
        ring = [None]
        for k in range(1, RADIUS + 1):
            ring.append(plane_at(src, p + k) + plane_at(src, p - k))
        weight = [-0.5 * a * w for w in stencil_weights]
        result = []
        for y in range(rows):
            v = cell[y]
            t = v * (a * pot[p, y : y + 1, :] + (3.0 * weight[0] + b))
            for k in range(1, RADIUS + 1):
                n = ring[k][:, y * cols : (y + 1) * cols]
                if y + k < rows:
                    n = n + cell[y + k]
                if y - k >= 0:
                    n = n + cell[y - k]
                n = n + jnp.where(col < cols - k, pltpu.roll(v, cols - k, 1), 0.0)
                n = n + jnp.where(col >= k, pltpu.roll(v, k, 1), 0.0)
                t = t + weight[k] * n
            result.append(t)
        return result

    def nonlocal_part(p, tiles):
        def atoms_of(j, tiles):
            tiles = list(tiles)
            for i in range(block):
                c = coef_wide[j * block + i]
                for y in range(rows):
                    tiles[y] = tiles[y] + c * proj[j * block + i, pl.ds(p * rows + y, 1), :]
            return tuple(tiles)

        return lax.fori_loop(0, atoms // block, atoms_of, tuple(tiles), unroll=atoms // block <= 2)

    def send_edges(k):
        base = halo_slots[k]
        to_up = remote(
            field.at[k, :, chunk * area : (chunk + RADIUS) * area], field.at[k, :, 0 : RADIUS * area], base, up
        )
        to_down = remote(
            field.at[k, :, RADIUS * area : 2 * RADIUS * area],
            field.at[k, :, (chunk + RADIUS) * area :], base + 1, down,
        )
        pl.when(has_up)(to_up.start)
        pl.when(has_down)(to_down.start)
        return to_up, to_down

    halo_slots = [slots(2) for _ in range(DEGREE + 1)]
    coef_slots = [slots(2) for _ in range(DEGREE + 1)]
    gram_slots = slots(2 + 2 * bands + 2 * bands + slabs)
    swap_slot, y_slot, h_slot = gram_slots, gram_slots + 2, gram_slots + 2 + bands
    r_slot, g_slot = gram_slots + 2 + 3 * bands, gram_slots + 2 + 4 * bands

    for copy in own:
        copy.wait()
    for copy in swaps:
        copy.wait_recv()

    halos = [send_edges(0)]
    waits = []
    for k in range(DEGREE + 1):
        final = k == DEGREE
        scale = 1.0 if final else (1.0 if k == 0 else 2.0) / filter_half
        shift = 0.0 if final else -filter_centre * scale
        src = field.at[k]

        def store(p, tiles):
            for y in range(rows):
                if final:
                    image[:, lanes(p * area + y * cols, cols)] = tiles[y]
                else:
                    field[k + 1, :, lanes((p + RADIUS) * area + y * cols, cols)] = tiles[y]

        def with_last(p, tiles):
            if final or k == 0:
                return tiles
            old = plane_at(field.at[k - 1], p)
            return [tiles[y] - old[:, y * cols : (y + 1) * cols] for y in range(rows)]

        coef_mine[k] = project(k)
        c_up = remote(coef_mine.at[k], coef_far.at[k, 0], coef_slots[k], up)
        c_down = remote(coef_mine.at[k], coef_far.at[k, 1], coef_slots[k] + 1, down)
        pl.when(has_up)(c_up.start)
        pl.when(has_down)(c_down.start)

        def inner(p, carry):
            store(p, with_last(p, local_part(src, p, scale, shift)))
            return carry

        lax.fori_loop(RADIUS, chunk - RADIUS, inner, 0)

        pl.when(has_down)(c_up.wait_recv)
        pl.when(has_up)(c_down.wait_recv)
        total = (coef_mine[k] + coef_far[k, 0] + coef_far[k, 1]) * (strength_ref[...] * scale)
        for a in range(atoms):
            coef_wide[a] = jnp.broadcast_to(total[:, a : a + 1], (half, cols))

        to_up, to_down = halos[k]
        pl.when(has_down)(to_up.wait_recv)
        pl.when(has_up)(to_down.wait_recv)

        def outer(n, carry):
            p = jnp.where(n < RADIUS, n, n + (chunk - 2 * RADIUS))
            store(p, nonlocal_part(p, with_last(p, local_part(src, p, scale, shift))))
            return carry

        lax.fori_loop(0, 2 * RADIUS, outer, 0)
        if not final:
            halos.append(send_edges(k + 1))

        def add_inner(p, carry):
            if final:
                old = image[:, lanes(p * area, area)]
            else:
                old = plane_at(field.at[k + 1], p)
            store(p, nonlocal_part(p, [old[:, y * cols : (y + 1) * cols] for y in range(rows)]))
            return carry

        lax.fori_loop(RADIUS, chunk - RADIUS, add_inner, 0)
        waits += [(has_up, c_up), (has_down, c_down), (has_up, to_up), (has_down, to_down)]

        if k == DEGREE - 1:
            mine_rows = pl.ds(pl.multiple_of(side * half, half), half)
            back = remote(
                field.at[DEGREE, :, lanes((RADIUS + other * planes) * area, planes * area)],
                slab_y.at[mine_rows], swap_slot, partner,
            )
            back.start()
            keep = pltpu.make_async_copy(field.at[DEGREE, :, here], slab_y.at[mine_rows], local.at[0])
            keep.start()

    states_all = bands * 2 * half
    share = planes // bands * area
    mine_h = pl.ds(pl.multiple_of(states_all + me_b * 2 * half + side * half, half), half)
    sent = []
    for d in range(bands):
        for e in range(2):
            to_b, to_s = lax.rem(me_b + d, bands), lax.rem(side + e, 2)
            part = image.at[:, lanes(to_s * planes * area + to_b * share, share)]
            if d == 0 and e == 0:
                keep_h = pltpu.make_async_copy(part, both.at[mine_h], local.at[1])
                keep_h.start()
            else:
                copy = remote(part, both.at[mine_h], h_slot + 2 * d + e, (to_b, 2 * pair + to_s))
                copy.start()
                sent.append(copy)
    keep.wait()
    back.wait_recv()
    mine_y = pl.ds(pl.multiple_of(me_b * 2 * half, half), 2 * half)
    for d in range(bands):
        to_b = lax.rem(me_b + d, bands)
        part = slab_y.at[:, lanes(to_b * share, share)]
        if d == 0:
            keep_y = pltpu.make_async_copy(part, both.at[mine_y], local.at[2])
            keep_y.start()
        else:
            copy = remote(part, both.at[mine_y], y_slot + d, (to_b, me_g))
            copy.start()
            sent.append(copy)
    out_copy = pltpu.make_async_copy(slab_y, out_ref, local.at[3])
    out_copy.start()
    keep_h.wait()
    keep_y.wait()
    for copy in sent:
        copy.wait_recv()

    everything = both[...]
    prod[...] = lax.dot_general(
        everything[:states_all], everything, (((1,), (1,)), ((), ())),
        precision=lax.Precision.HIGHEST, preferred_element_type=jnp.float32,
    )
    rows_of = 2 * half
    band_copies = []
    for d in range(1, bands):
        to_b = lax.rem(me_b + d, bands)
        copy = remote(
            prod.at[pl.ds(pl.multiple_of(to_b * rows_of, rows_of), rows_of)], band_sum.at[me_b],
            r_slot + d, (to_b, me_g),
        )
        copy.start()
        band_copies.append(copy)
    total = prod[pl.ds(pl.multiple_of(me_b * rows_of, rows_of), rows_of), :]
    for copy in band_copies:
        copy.wait_recv()
    for d in range(1, bands):
        total = total + band_sum[lax.rem(me_b + d, bands)]
    mine[...] = total
    grid_copies = []
    for d in range(1, slabs):
        copy = remote(mine, grid_sum.at[d], g_slot + d, (me_b, lax.rem(me_g + d, slabs)))
        copy.start()
        grid_copies.append(copy)
    for copy in grid_copies:
        copy.wait_recv()
    for d in range(1, slabs):
        total = total + grid_sum[d]
    total = total / total_points
    gram_ref[...] = total[:, :states_all]
    ham_ref[...] = total[:, states_all:]

    for copy in swaps + [back] + sent + band_copies + grid_copies:
        copy.wait_send()
    for ready, copy in waits:
        pl.when(ready)(copy.wait_send)
    out_copy.wait()


def per_device(bands, slabs, states, potential, proj_index, proj_value, proj_strength):
    state_count, planes, rows, cols = states.shape
    area = rows * cols
    points = planes * area
    atoms = proj_index.shape[0]
    half = state_count // 2
    chunk = 2 * planes
    wide = -(-atoms // LANES) * LANES
    all_states = bands * state_count
    share = planes // bands * area
    strength = jnp.pad(proj_strength, (0, wide - atoms)).reshape(1, wide)
    slots = 2 + 4 * (DEGREE + 1) + 2 + 4 * bands + slabs
    vmem, hbm = pl.BlockSpec(memory_space=pltpu.VMEM), pl.BlockSpec(memory_space=pl.ANY)
    f32 = jnp.float32
    out, gram, ham = pl.pallas_call(
        functools.partial(
            kernel, bands, slabs, planes, rows, cols, atoms, float(points * slabs)
        ),
        out_shape=(
            jax.ShapeDtypeStruct((state_count, points), f32),
            jax.ShapeDtypeStruct((state_count, all_states), f32),
            jax.ShapeDtypeStruct((state_count, all_states), f32),
        ),
        in_specs=[hbm, vmem, vmem, vmem, vmem],
        out_specs=(hbm, vmem, vmem),
        scratch_shapes=[
            pltpu.VMEM((DEGREE + 1, half, (chunk + 2 * RADIUS) * area), f32),
            pltpu.VMEM((half, chunk * area), f32),
            pltpu.VMEM((chunk, rows, cols), f32),
            pltpu.VMEM((atoms, chunk * rows, cols), f32),
            pltpu.VMEM((DEGREE + 1, half, wide), f32),
            pltpu.VMEM((DEGREE + 1, 2, half, wide), f32),
            pltpu.VMEM((atoms, half, cols), f32),
            pltpu.VMEM((state_count, points), f32),
            pltpu.VMEM((2 * all_states, share), f32),
            pltpu.VMEM((all_states, 2 * all_states), f32),
            pltpu.VMEM((bands, state_count, 2 * all_states), f32),
            pltpu.VMEM((state_count, 2 * all_states), f32),
            pltpu.VMEM((slabs, state_count, 2 * all_states), f32),
            pltpu.SemaphoreType.DMA((slots,)),
            pltpu.SemaphoreType.DMA((slots,)),
            pltpu.SemaphoreType.DMA((4,)),
        ],
        compiler_params=pltpu.CompilerParams(
            collective_id=0, has_side_effects=True, vmem_limit_bytes=48 * 1024 * 1024
        ),
    )(states.reshape(state_count, points), potential, proj_index, proj_value, strength)
    return out.reshape(states.shape), gram, ham


def solution(mesh):
    in_specs = (P("band", "grid", None, None), P("grid", None, None), P(), P(), P())
    out_specs = (P("band", "grid", None, None), P("band", None), P("band", None))
    return jax.shard_map(
        functools.partial(per_device, mesh.shape["band"], mesh.shape["grid"]),
        mesh=mesh, in_specs=in_specs, out_specs=out_specs, check_vma=False,
    )
```

time: 212 us -> 64.8 us (0.31)
  blocking collectives: 138 us -> 0 us
  Pallas kernels: 0 us -> 59.8 us
  other arithmetic: 24.2 us -> 0 us
  starting transfers between devices: 17.3 us -> 0 us
  between operations: 14.5 us -> 0.68 us
  matrix products: 13.6 us -> 0 us
    psum x6 -> x0, blocking collectives: 138 us -> none  [the longest x5 105 us: apply_h(): coeffs = lax.psum(partial_value, 'grid')]
    pallas_call x0 -> x1, Pallas kernels: none -> 59.8 us  [per_device(): pl.pallas_call(functools.partial(kernel, bands, slabs, planes, rows, cols...]
    ppermute x10 -> x0, starting transfers between devices: 17.2 us -> none  [the longest x5 10.8 us: padded_2(): lax.ppermute(lax.slice_in_dim(block, block.shape[dim] - width, None, axis...]
    unnamed x4 -> x0, other arithmetic: 15.8 us -> none
    dot_general x12 -> x0, matrix products: 13.6 us -> none  [the longest x7 10.1 us: inner_rows(): lax.dot_general(left, right, (((1,), (1,)), ((), ())), precision=lax.Prec...]
    sub x3 -> x0, other arithmetic: 3.89 us -> none  [per_device(): 2.0 * (apply_h(current) - filter_centre * current) / filter_half - previous]
    unnamed x18 -> x12, local copies, waits for them, and re-layouts: 1.78 us -> 4.13 us
  transfers between devices with their start and end apart: 11 -> 0, of which waited for: 0 -> 0; matrix products, arithmetic and copies ran while one was open for 13% -> 0% of each run, Pallas kernels for 0% -> 0%
where the time goes in v1:
time: 64.8 us; the launch traced here: 64.6 us
  Pallas kernels  59.8 us (92%)
  local copies, waits for them, and re-layouts  4.14 us (6%)
  between operations  0.68 us (1%)
    pallas_call x1, Pallas kernels, per_device(): pl.pallas_call(functools.partial(kernel, bands, slabs, planes, rows, cols...  59.8 us
    unnamed x12, local copies, waits for them, and re-layouts  4.13 us

profile of v1, /device:TPU:0, one launch (start us, length us, event | category | flops | bytes accessed | tf_op | source)
XLA Modules:
  0.0 64.6 jit_solution(17318346396625026922)
XLA Ops:
  0.6 0.0 copy-start.3
  0.6 0.6 copy-done.3
  1.3 0.0 copy-start
  1.3 0.0 copy-start.1
  1.3 0.0 copy-start.2
  1.3 1.4 %copy.11 = f32[2,8,64,128]{3,1,2,0:T(8,128)S(1)} copy(f32[2,8,64,128]{3,2,1,0:T(8,128)} %bitcast.12) | data formatting | bytes 1048576
  2.7 0.0 copy-done
  2.7 0.0 copy-done.1
  2.7 0.0 copy-done.2
  2.7 59.8 %shard_map.76 = (f32[16,8192]{1,0:T(8,128)S(1)}, f32[16,64]{1,0:T(8,128)S(1)}, f32[16,64]{1,0:T(8,128)S(1)}) custom-call(f32[16,8192]{1,0:T(8,128)S(1)} %bitcast.10, f32[8,8,128]{2,1,0:T(8,128)S(1)} %copy-done, s32[16,128]{1,0:T(8,128)S(1)} %copy-done.1, f32[16,128]{1,0:T(8,128)S(1)} %copy-done.2, f32[1,128]{1,0:T(1,128)S(1)} %pad_bitcast_fusion.strength_ref), custom_call_target="tpu_custom_call" | custom-call | tf_op jit(solution)/shard_map/pallas_call | solution.py:351
  62.6 0.9 %copy.9 = f32[2,8,64,128]{3,2,1,0:T(8,128)} copy(f32[2,8,64,128]{3,1,2,0:T(8,128)S(1)} %bitcast.11) | data formatting | bytes 1048576
  63.5 0.6 copy.14
  64.0 0.6 copy.15
  (1 shorter events, 0.0 us)
Async XLA Ops:
  0.6 0.7 %copy-start.3 = (f32[16]{0:T(128)S(1)}, f32[16]{0:T(128)}, u32[]{:S(2)}) copy-start(f32[16]{0:T(128)} %param.9) | copy-start | bytes 196
  1.3 1.4 %copy-start = (f32[8,8,128]{2,1,0:T(8,128)S(1)}, f32[8,8,128]{2,1,0:T(8,128)}, u32[]{:S(2)}) copy-start(f32[8,8,128]{2,1,0:T(8,128)} %potential.1) | copy-start | bytes 98308
  1.3 1.4 %copy-start.1 = (s32[16,128]{1,0:T(8,128)S(1)}, s32[16,128]{1,0:T(8,128)}, u32[]{:S(2)}) copy-start(s32[16,128]{1,0:T(8,128)} %index_ref.1) | copy-start | bytes 24580
  1.3 1.4 %copy-start.2 = (f32[16,128]{1,0:T(8,128)S(1)}, f32[16,128]{1,0:T(8,128)}, u32[]{:S(2)}) copy-start(f32[16,128]{1,0:T(8,128)} %value_ref.1) | copy-start | bytes 24580

commit v2 on v1

--- a/solution.py
+++ b/solution.py
@@ -21,7 +21,7 @@
     bands, slabs, planes, rows, cols, atoms, total_points,
     states, potential, index_ref, value_ref, strength_ref,
     out_ref, gram_ref, ham_ref,
-    field, image, pot, proj, coef_mine, coef_far, coef_wide, slab_y, both, prod, band_sum, mine, grid_sum,
+    raw, field, image, pot, proj, coef_mine, coef_far, coef_wide, slab_y, both, prod, band_sum, mine, grid_sum,
     send, recv, local,
 ):
     half = states.shape[0] // 2
@@ -53,34 +53,58 @@
         field[k, :, (RADIUS + chunk) * area :] = jnp.zeros((half, RADIUS * area), jnp.float32)
     coef_far[...] = jnp.zeros_like(coef_far)
 
-    barrier = pltpu.get_barrier_semaphore()
-    peers = [(me_b, lax.rem(me_g + d, slabs)) for d in range(1, slabs)]
+    partner = (me_b, 2 * pair + other)
+    up, down = (me_b, me_g + 2), (me_b, me_g - 2)
     crossing = [
         (lax.rem(me_b + d, bands), 2 * pair + lax.rem(side + e, 2)) for d in range(1, bands) for e in range(2)
     ]
-    for peer in peers + crossing:
-        pl.semaphore_signal(barrier, inc=1, device_id=peer, device_id_type=MESH)
-    pl.semaphore_wait(barrier, len(peers) + len(crossing))
-
-    partner = (me_b, 2 * pair + other)
-    up, down = (me_b, me_g + 2), (me_b, me_g - 2)
+    barrier = pltpu.get_barrier_semaphore()
+
+    def greet(where):
+        pl.semaphore_signal(barrier, inc=1, device_id=where, device_id_type=MESH)
+
+    for peer in crossing:
+        greet(peer)
+    if last_pair > DEGREE:
+        for d in range(1, slabs):
+            greet((me_b, lax.rem(me_g + d, slabs)))
+        expected = len(crossing) + slabs - 1
+    else:
+        greet(partner)
+        pl.when(has_up)(lambda: greet(up))
+        pl.when(has_down)(lambda: greet(down))
+        expected = len(crossing) + 1 + has_up.astype(jnp.int32) + has_down.astype(jnp.int32)
+
+    pl.semaphore_wait(barrier, expected)
 
     here = lanes((RADIUS + side * planes) * area, planes * area)
-    first = slots(2)
+    outer_at, inner_at = side * (planes - RADIUS), other * RADIUS
+    theirs = pl.ds(pl.multiple_of(other * half, half), half)
+    first = slots(3)
+
+    def piece(slot, start, count):
+        return remote(
+            states.at[theirs, pl.ds(pl.multiple_of(start * rows, rows), count * rows)],
+            raw.at[:, pl.ds(pl.multiple_of((side * planes + start) * rows, rows), count * rows)], slot, partner,
+        )
+
     swaps = [
-        remote(potential, pot.at[pl.ds(side * planes, planes)], first, partner),
-        remote(states.at[pl.ds(pl.multiple_of(other * half, half), half)], field.at[0, :, here], first + 1, partner),
+        piece(first, outer_at, RADIUS),
+        piece(first + 1, inner_at, planes - RADIUS),
+        remote(potential, pot.at[pl.ds(side * planes, planes)], first + 2, partner),
     ]
     for copy in swaps:
         copy.start()
     own = [
+        pltpu.make_async_copy(
+            states.at[pl.ds(pl.multiple_of(side * half, half), half)],
+            raw.at[:, pl.ds(pl.multiple_of(side * planes * rows, rows), planes * rows)], local.at[1]
+        ),
         pltpu.make_async_copy(potential, pot.at[pl.ds(side * planes, planes)], local.at[0]),
-        pltpu.make_async_copy(
-            states.at[pl.ds(pl.multiple_of(side * half, half), half)], field.at[0, :, here], local.at[1]
-        ),
     ]
     for copy in own:
         copy.start()
+
 
     points = index_ref.shape[1]
     row_iota = lax.broadcasted_iota(jnp.int32, (chunk * rows, points), 0) + pair * (chunk * rows)
@@ -99,7 +123,6 @@
         return carry
 
     lax.fori_loop(0, atoms, build, 0)
-
     col = lax.broadcasted_iota(jnp.int32, (half, cols), 1)
     wide = coef_mine.shape[-1]
     wide_iota = lax.broadcasted_iota(jnp.int32, (half, wide), 1)
@@ -127,24 +150,26 @@
 
         return lax.fori_loop(0, atoms // block, atoms_of, jnp.zeros((half, wide), jnp.float32))
 
-    def local_part(src, p, a, b):
+    def local_part(src, p, a, b, low=chunk, high=chunk):
         c = plane_at(src, p)
         cell = [c[:, y * cols : (y + 1) * cols] for y in range(rows)]
         ring = [None]
         for k in range(1, RADIUS + 1):
-            ring.append(plane_at(src, p + k) + plane_at(src, p - k))
+            near = [plane_at(src, p + s * k) for s, room in ((1, high), (-1, low)) if k <= room]
+            ring.append(near[0] + near[1] if len(near) == 2 else near[0] if near else None)
         weight = [-0.5 * a * w for w in stencil_weights]
         result = []
         for y in range(rows):
             v = cell[y]
             t = v * (a * pot[p, y : y + 1, :] + (3.0 * weight[0] + b))
             for k in range(1, RADIUS + 1):
-                n = ring[k][:, y * cols : (y + 1) * cols]
+                n = jnp.where(col < cols - k, pltpu.roll(v, cols - k, 1), 0.0)
+                if ring[k] is not None:
+                    n = n + ring[k][:, y * cols : (y + 1) * cols]
                 if y + k < rows:
                     n = n + cell[y + k]
                 if y - k >= 0:
                     n = n + cell[y - k]
-                n = n + jnp.where(col < cols - k, pltpu.roll(v, cols - k, 1), 0.0)
                 n = n + jnp.where(col >= k, pltpu.roll(v, k, 1), 0.0)
                 t = t + weight[k] * n
             result.append(t)
@@ -161,7 +186,7 @@
 
         return lax.fori_loop(0, atoms // block, atoms_of, tuple(tiles), unroll=atoms // block <= 2)
 
-    def send_edges(k):
+    def edges(k):
         base = halo_slots[k]
         to_up = remote(
             field.at[k, :, chunk * area : (chunk + RADIUS) * area], field.at[k, :, 0 : RADIUS * area], base, up
@@ -170,8 +195,6 @@
             field.at[k, :, RADIUS * area : 2 * RADIUS * area],
             field.at[k, :, (chunk + RADIUS) * area :], base + 1, down,
         )
-        pl.when(has_up)(to_up.start)
-        pl.when(has_down)(to_down.start)
         return to_up, to_down
 
     halo_slots = [slots(2) for _ in range(DEGREE + 1)]
@@ -180,12 +203,30 @@
     swap_slot, y_slot, h_slot = gram_slots, gram_slots + 2, gram_slots + 2 + bands
     r_slot, g_slot = gram_slots + 2 + 3 * bands, gram_slots + 2 + 4 * bands
 
-    for copy in own:
-        copy.wait()
-    for copy in swaps:
-        copy.wait_recv()
-
-    halos = [send_edges(0)]
+    def relayout(start, count):
+        def at_plane(n, carry):
+            p = start + n
+            cube = jnp.swapaxes(raw[:, pl.ds(pl.multiple_of(p * rows, rows), rows), :], 0, 1)
+            for y in range(rows):
+                field[0, :, lanes((p + RADIUS) * area + y * cols, cols)] = cube[y]
+            return carry
+
+        lax.fori_loop(0, count, at_plane, 0)
+
+    halos = [edges(0)]
+    own[0].wait()
+    relayout(side * planes, planes)
+    pl.when(has_up & (side == 1))(halos[0][0].start)
+    pl.when(has_down & (side == 0))(halos[0][1].start)
+    swaps[0].wait_recv()
+    relayout(other * (chunk - RADIUS), RADIUS)
+    pl.when(has_up & (side == 0))(halos[0][0].start)
+    pl.when(has_down & (side == 1))(halos[0][1].start)
+    own[1].wait()
+    swaps[1].wait_recv()
+    relayout(RADIUS + other * (planes - RADIUS), planes - RADIUS)
+    swaps[2].wait_recv()
+
     waits = []
     for k in range(DEGREE + 1):
         final = k == DEGREE
@@ -217,35 +258,47 @@
             return carry
 
         lax.fori_loop(RADIUS, chunk - RADIUS, inner, 0)
+        for n in range(RADIUS):
+            for p, low, high in ((n, n, chunk), (chunk - 1 - n, chunk, n)):
+                store(p, with_last(p, local_part(src, p, scale, shift, low, high)))
 
         pl.when(has_down)(c_up.wait_recv)
         pl.when(has_up)(c_down.wait_recv)
-        total = (coef_mine[k] + coef_far[k, 0] + coef_far[k, 1]) * (strength_ref[...] * scale)
+        total = (coef_mine[k] + coef_far[k, 0] + coef_far[k, 1]) * scale
         for a in range(atoms):
-            coef_wide[a] = jnp.broadcast_to(total[:, a : a + 1], (half, cols))
+            coef_wide[a] = jnp.broadcast_to(total[:, a : a + 1] * strength_ref[:, a : a + 1], (half, cols))
+
+        def stored(p):
+            old = image[:, lanes(p * area, area)] if final else plane_at(field.at[k + 1], p)
+            return [old[:, y * cols : (y + 1) * cols] for y in range(rows)]
+
+        def add_nonlocal(p, carry):
+            store(p, nonlocal_part(p, stored(p)))
+            return carry
+
+        lax.fori_loop(0, chunk, add_nonlocal, 0)
 
         to_up, to_down = halos[k]
+
+        def add_halo(p, planes_in):
+            tiles = stored(p)
+            for w, plane in planes_in:
+                far = src[:, plane * area : (plane + 1) * area]
+                tiles = [t + (-0.5 * scale * w) * far[:, y * cols : (y + 1) * cols] for y, t in enumerate(tiles)]
+            store(p, tiles)
+
         pl.when(has_down)(to_up.wait_recv)
+        for p in range(RADIUS):
+            add_halo(p, [(stencil_weights[d], RADIUS + p - d) for d in range(p + 1, RADIUS + 1)])
+        if not final:
+            halos.append(edges(k + 1))
+            pl.when(has_down)(halos[-1][1].start)
         pl.when(has_up)(to_down.wait_recv)
-
-        def outer(n, carry):
-            p = jnp.where(n < RADIUS, n, n + (chunk - 2 * RADIUS))
-            store(p, nonlocal_part(p, with_last(p, local_part(src, p, scale, shift))))
-            return carry
-
-        lax.fori_loop(0, 2 * RADIUS, outer, 0)
+        for n in range(RADIUS):
+            p = chunk - 1 - n
+            add_halo(p, [(stencil_weights[d], RADIUS + p + d) for d in range(n + 1, RADIUS + 1)])
         if not final:
-            halos.append(send_edges(k + 1))
-
-        def add_inner(p, carry):
-            if final:
-                old = image[:, lanes(p * area, area)]
-            else:
-                old = plane_at(field.at[k + 1], p)
-            store(p, nonlocal_part(p, [old[:, y * cols : (y + 1) * cols] for y in range(rows)]))
-            return carry
-
-        lax.fori_loop(RADIUS, chunk - RADIUS, add_inner, 0)
+            pl.when(has_up)(halos[-1][0].start)
         waits += [(has_up, c_up), (has_down, c_down), (has_up, to_up), (has_down, to_down)]
 
         if k == DEGREE - 1:
@@ -261,7 +314,7 @@
     states_all = bands * 2 * half
     share = planes // bands * area
     mine_h = pl.ds(pl.multiple_of(states_all + me_b * 2 * half + side * half, half), half)
-    sent = []
+    sent_h, sent_y = [], []
     for d in range(bands):
         for e in range(2):
             to_b, to_s = lax.rem(me_b + d, bands), lax.rem(side + e, 2)
@@ -272,7 +325,7 @@
             else:
                 copy = remote(part, both.at[mine_h], h_slot + 2 * d + e, (to_b, 2 * pair + to_s))
                 copy.start()
-                sent.append(copy)
+                sent_h.append(copy)
     keep.wait()
     back.wait_recv()
     mine_y = pl.ds(pl.multiple_of(me_b * 2 * half, half), 2 * half)
@@ -285,19 +338,23 @@
         else:
             copy = remote(part, both.at[mine_y], y_slot + d, (to_b, me_g))
             copy.start()
-            sent.append(copy)
-    out_copy = pltpu.make_async_copy(slab_y, out_ref, local.at[3])
-    out_copy.start()
+            sent_y.append(copy)
+    keep_y.wait()
+    for copy in sent_y:
+        copy.wait_recv()
+
+    def inner_rows(left, right):
+        return lax.dot_general(
+            left, right, (((1,), (1,)), ((), ())),
+            precision=lax.Precision.HIGHEST, preferred_element_type=jnp.float32,
+        )
+
+    all_y = both[:states_all, :]
+    prod[:, :states_all] = inner_rows(all_y, all_y)
     keep_h.wait()
-    keep_y.wait()
-    for copy in sent:
+    for copy in sent_h:
         copy.wait_recv()
-
-    everything = both[...]
-    prod[...] = lax.dot_general(
-        everything[:states_all], everything, (((1,), (1,)), ((), ())),
-        precision=lax.Precision.HIGHEST, preferred_element_type=jnp.float32,
-    )
+    prod[:, states_all:] = inner_rows(both[:states_all, :], both[states_all:, :])
     rows_of = 2 * half
     band_copies = []
     for d in range(1, bands):
@@ -319,6 +376,15 @@
         copy = remote(mine, grid_sum.at[d], g_slot + d, (me_b, lax.rem(me_g + d, slabs)))
         copy.start()
         grid_copies.append(copy)
+
+    def put_out(p, carry):
+        for g in range(2):
+            v = slab_y[g * half : (g + 1) * half, lanes(p * area, area)]
+            cube = jnp.stack([v[:, y * cols : (y + 1) * cols] for y in range(rows)])
+            out_ref[g * half : (g + 1) * half, pl.ds(pl.multiple_of(p * rows, rows), rows), :] = jnp.swapaxes(cube, 0, 1)
+        return carry
+
+    lax.fori_loop(0, planes, put_out, 0)
     for copy in grid_copies:
         copy.wait_recv()
     for d in range(1, slabs):
@@ -327,11 +393,10 @@
     gram_ref[...] = total[:, :states_all]
     ham_ref[...] = total[:, states_all:]
 
-    for copy in swaps + [back] + sent + band_copies + grid_copies:
+    for copy in swaps + [back] + sent_h + sent_y + band_copies + grid_copies:
         copy.wait_send()
     for ready, copy in waits:
         pl.when(ready)(copy.wait_send)
-    out_copy.wait()
 
 
 def per_device(bands, slabs, states, potential, proj_index, proj_value, proj_strength):
@@ -344,8 +409,8 @@
     wide = -(-atoms // LANES) * LANES
     all_states = bands * state_count
     share = planes // bands * area
-    strength = jnp.pad(proj_strength, (0, wide - atoms)).reshape(1, wide)
-    slots = 2 + 4 * (DEGREE + 1) + 2 + 4 * bands + slabs
+    strength = proj_strength.reshape(1, atoms)
+    slots = 3 + 4 * (DEGREE + 1) + 2 + 4 * bands + slabs
     vmem, hbm = pl.BlockSpec(memory_space=pltpu.VMEM), pl.BlockSpec(memory_space=pl.ANY)
     f32 = jnp.float32
     out, gram, ham = pl.pallas_call(
@@ -353,13 +418,14 @@
             kernel, bands, slabs, planes, rows, cols, atoms, float(points * slabs)
         ),
         out_shape=(
-            jax.ShapeDtypeStruct((state_count, points), f32),
+            jax.ShapeDtypeStruct((state_count, planes * rows, cols), f32),
             jax.ShapeDtypeStruct((state_count, all_states), f32),
             jax.ShapeDtypeStruct((state_count, all_states), f32),
         ),
         in_specs=[hbm, vmem, vmem, vmem, vmem],
-        out_specs=(hbm, vmem, vmem),
+        out_specs=(vmem, vmem, vmem),
         scratch_shapes=[
+            pltpu.VMEM((half, chunk * rows, cols), f32),
             pltpu.VMEM((DEGREE + 1, half, (chunk + 2 * RADIUS) * area), f32),
             pltpu.VMEM((half, chunk * area), f32),
             pltpu.VMEM((chunk, rows, cols), f32),
@@ -380,7 +446,7 @@
         compiler_params=pltpu.CompilerParams(
             collective_id=0, has_side_effects=True, vmem_limit_bytes=48 * 1024 * 1024
         ),
-    )(states.reshape(state_count, points), potential, proj_index, proj_value, strength)
+    )(states.reshape(state_count, planes * rows, cols), potential, proj_index, proj_value, strength)
     return out.reshape(states.shape), gram, ham
 
 

time: 64.8 us -> 64.1 us (0.989)
  Pallas kernels: 59.8 us -> 57.3 us
  local copies, waits for them, and re-layouts: 4.14 us -> 5.83 us
    pallas_call x1, Pallas kernels: 59.8 us -> 57.3 us  [per_device(): pl.pallas_call(functools.partial(kernel, bands, slabs, planes, rows, cols...]
    unnamed x12 -> x13, local copies, waits for them, and re-layouts: 4.13 us -> 5.83 us
where the time goes in v2:
time: 64.1 us; the launch traced here: 63.8 us
  Pallas kernels  57.3 us (89%)
  local copies, waits for them, and re-layouts  5.83 us (9%)
  between operations  0.65 us (1%)
    pallas_call x1, Pallas kernels, per_device(): pl.pallas_call(functools.partial(kernel, bands, slabs, planes, rows, cols...  57.3 us
    unnamed x13, local copies, waits for them, and re-layouts  5.83 us

profile of v2, /device:TPU:0, one launch (start us, length us, event | category | flops | bytes accessed | tf_op | source)
XLA Modules:
  0.0 63.8 jit_solution(18326909591652430977)
XLA Ops:
  0.6 0.0 copy-start.4
  0.6 0.6 %copy-done.4 = f32[16]{0:T(128)S(1)} copy-done((f32[16]{0:T(128)S(1)}, f32[16]{0:T(128)}, u32[]{:S(2)}) %copy-start.4) | copy-done | bytes 88
  1.3 0.0 copy-start
  1.3 1.0 %copy-done = f32[16,8,8,128]{3,2,1,0:T(8,128)S(1)} copy-done((f32[16,8,8,128]{3,2,1,0:T(8,128)S(1)}, f32[16,8,8,128]{3,2,1,0:T(8,128)}, u32[]{:S(2)}) %copy-start) | copy-done | bytes 524312
  2.3 0.0 copy-start.1
  2.3 0.8 %copy-done.1 = f32[8,8,128]{2,1,0:T(8,128)S(1)} copy-done((f32[8,8,128]{2,1,0:T(8,128)S(1)}, f32[8,8,128]{2,1,0:T(8,128)}, u32[]{:S(2)}) %copy-start.1) | copy-done | bytes 32792
  3.1 0.0 copy-start.2
  3.1 0.7 %copy-done.2 = s32[16,128]{1,0:T(8,128)S(1)} copy-done((s32[16,128]{1,0:T(8,128)S(1)}, s32[16,128]{1,0:T(8,128)}, u32[]{:S(2)}) %copy-start.2) | copy-done | bytes 8216
  3.8 0.0 copy-start.3
  3.8 0.7 %copy-done.3 = f32[16,128]{1,0:T(8,128)S(1)} copy-done((f32[16,128]{1,0:T(8,128)S(1)}, f32[16,128]{1,0:T(8,128)}, u32[]{:S(2)}) %copy-start.3) | copy-done | bytes 8216
  4.5 57.3 %shard_map.76 = (f32[16,64,128]{2,1,0:T(8,128)S(1)}, f32[16,64]{1,0:T(8,128)S(1)}, f32[16,64]{1,0:T(8,128)S(1)}) custom-call(f32[16,64,128]{2,1,0:T(8,128)S(1)} %bitcast.3, f32[8,8,128]{2,1,0:T(8,128)S(1)} %copy-done.1, s32[16,128]{1,0:T(8,128)S(1)} %copy-done.2, f32[16,128]{1,0:T(8,128)S(1)} %copy-done.3, f32[1,16]{1,0:T(1,128)S(1)} %bitcast.5), custom_call_target="tpu_custom_call" | custom-call | tf_op jit(solution)/shard_map/pallas_call | solution.py:416
  61.8 0.8 %copy.11 = f32[16,8,8,128]{3,2,1,0:T(8,128)} copy(f32[16,8,8,128]{3,2,1,0:T(8,128)S(1)} %bitcast.4) | data formatting | bytes 1048576
  62.6 0.6 copy.12
  63.2 0.6 copy.13
Async XLA Ops:
  0.6 0.7 %copy-start.4 = (f32[16]{0:T(128)S(1)}, f32[16]{0:T(128)}, u32[]{:S(2)}) copy-start(f32[16]{0:T(128)} %param.9) | copy-start | bytes 196
  1.3 1.0 %copy-start = (f32[16,8,8,128]{3,2,1,0:T(8,128)S(1)}, f32[16,8,8,128]{3,2,1,0:T(8,128)}, u32[]{:S(2)}) copy-start(f32[16,8,8,128]{3,2,1,0:T(8,128)} %param.5) | copy-start | bytes 1572868
  2.3 0.8 %copy-start.1 = (f32[8,8,128]{2,1,0:T(8,128)S(1)}, f32[8,8,128]{2,1,0:T(8,128)}, u32[]{:S(2)}) copy-start(f32[8,8,128]{2,1,0:T(8,128)} %potential.1) | copy-start | bytes 98308
  3.1 0.7 %copy-start.2 = (s32[16,128]{1,0:T(8,128)S(1)}, s32[16,128]{1,0:T(8,128)}, u32[]{:S(2)}) copy-start(s32[16,128]{1,0:T(8,128)} %index_ref.1) | copy-start | bytes 24580
  3.8 0.7 %copy-start.3 = (f32[16,128]{1,0:T(8,128)S(1)}, f32[16,128]{1,0:T(8,128)}, u32[]{:S(2)}) copy-start(f32[16,128]{1,0:T(8,128)} %value_ref.1) | copy-start | bytes 24580

commit v3 on v2

--- a/solution.py
+++ b/solution.py
@@ -199,9 +199,9 @@
 
     halo_slots = [slots(2) for _ in range(DEGREE + 1)]
     coef_slots = [slots(2) for _ in range(DEGREE + 1)]
-    gram_slots = slots(2 + 2 * bands + 2 * bands + slabs)
+    gram_slots = slots(2 + 2 * bands + 3 * bands + slabs)
     swap_slot, y_slot, h_slot = gram_slots, gram_slots + 2, gram_slots + 2 + bands
-    r_slot, g_slot = gram_slots + 2 + 3 * bands, gram_slots + 2 + 4 * bands
+    r_slot, e_slot, g_slot = (gram_slots + 2 + n * bands for n in (3, 4, 5))
 
     def relayout(start, count):
         def at_plane(n, carry):
@@ -227,7 +227,8 @@
     relayout(RADIUS + other * (planes - RADIUS), planes - RADIUS)
     swaps[2].wait_recv()
 
-    waits = []
+    waits, sent_y = [], []
+    share = planes // bands * area
     for k in range(DEGREE + 1):
         final = k == DEGREE
         scale = 1.0 if final else (1.0 if k == 0 else 2.0) / filter_half
@@ -310,11 +311,19 @@
             back.start()
             keep = pltpu.make_async_copy(field.at[DEGREE, :, here], slab_y.at[mine_rows], local.at[0])
             keep.start()
+            for d in range(1, bands):
+                to_b = lax.rem(me_b + d, bands)
+                copy = remote(
+                    field.at[DEGREE, :, lanes((RADIUS + side * planes) * area + to_b * share, share)],
+                    both.at[pl.ds(pl.multiple_of(me_b * 2 * half + side * half, half), half)],
+                    e_slot + d, (to_b, me_g),
+                )
+                copy.start()
+                sent_y.append(copy)
 
     states_all = bands * 2 * half
-    share = planes // bands * area
     mine_h = pl.ds(pl.multiple_of(states_all + me_b * 2 * half + side * half, half), half)
-    sent_h, sent_y = [], []
+    sent_h = []
     for d in range(bands):
         for e in range(2):
             to_b, to_s = lax.rem(me_b + d, bands), lax.rem(side + e, 2)
@@ -331,12 +340,16 @@
     mine_y = pl.ds(pl.multiple_of(me_b * 2 * half, half), 2 * half)
     for d in range(bands):
         to_b = lax.rem(me_b + d, bands)
-        part = slab_y.at[:, lanes(to_b * share, share)]
         if d == 0:
+            part = slab_y.at[:, lanes(to_b * share, share)]
             keep_y = pltpu.make_async_copy(part, both.at[mine_y], local.at[2])
             keep_y.start()
         else:
-            copy = remote(part, both.at[mine_y], y_slot + d, (to_b, me_g))
+            copy = remote(
+                slab_y.at[pl.ds(pl.multiple_of(other * half, half), half), lanes(to_b * share, share)],
+                both.at[pl.ds(pl.multiple_of(me_b * 2 * half + other * half, half), half)],
+                y_slot + d, (to_b, me_g),
+            )
             copy.start()
             sent_y.append(copy)
     keep_y.wait()
@@ -410,7 +423,7 @@
     all_states = bands * state_count
     share = planes // bands * area
     strength = proj_strength.reshape(1, atoms)
-    slots = 3 + 4 * (DEGREE + 1) + 2 + 4 * bands + slabs
+    slots = 3 + 4 * (DEGREE + 1) + 2 + 5 * bands + slabs
     vmem, hbm = pl.BlockSpec(memory_space=pltpu.VMEM), pl.BlockSpec(memory_space=pl.ANY)
     f32 = jnp.float32
     out, gram, ham = pl.pallas_call(

time: 64.1 us -> 62.9 us (0.981)
  Pallas kernels: 57.3 us -> 56.1 us
    pallas_call x1, Pallas kernels: 57.3 us -> 56.1 us  [per_device(): pl.pallas_call(functools.partial(kernel, bands, slabs, planes, rows, cols...]
where the time goes in v3:
time: 62.9 us; the launch traced here: 62.6 us
  Pallas kernels  56.1 us (89%)
  local copies, waits for them, and re-layouts  5.83 us (9%)
  between operations  0.65 us (1%)
    pallas_call x1, Pallas kernels, per_device(): pl.pallas_call(functools.partial(kernel, bands, slabs, planes, rows, cols...  56.1 us
    unnamed x13, local copies, waits for them, and re-layouts  5.83 us

profile of v3, /device:TPU:0, one launch (start us, length us, event | category | flops | bytes accessed | tf_op | source)
XLA Modules:
  0.0 62.6 jit_solution(2195190898480100832)
XLA Ops:
  0.6 0.0 copy-start.4
  0.6 0.6 %copy-done.4 = f32[16]{0:T(128)S(1)} copy-done((f32[16]{0:T(128)S(1)}, f32[16]{0:T(128)}, u32[]{:S(2)}) %copy-start.4) | copy-done | bytes 88
  1.3 0.0 copy-start
  1.3 1.0 %copy-done = f32[16,8,8,128]{3,2,1,0:T(8,128)S(1)} copy-done((f32[16,8,8,128]{3,2,1,0:T(8,128)S(1)}, f32[16,8,8,128]{3,2,1,0:T(8,128)}, u32[]{:S(2)}) %copy-start) | copy-done | bytes 524312
  2.3 0.0 copy-start.1
  2.3 0.8 %copy-done.1 = f32[8,8,128]{2,1,0:T(8,128)S(1)} copy-done((f32[8,8,128]{2,1,0:T(8,128)S(1)}, f32[8,8,128]{2,1,0:T(8,128)}, u32[]{:S(2)}) %copy-start.1) | copy-done | bytes 32792
  3.1 0.0 copy-start.2
  3.1 0.7 %copy-done.2 = s32[16,128]{1,0:T(8,128)S(1)} copy-done((s32[16,128]{1,0:T(8,128)S(1)}, s32[16,128]{1,0:T(8,128)}, u32[]{:S(2)}) %copy-start.2) | copy-done | bytes 8216
  3.8 0.0 copy-start.3
  3.8 0.7 %copy-done.3 = f32[16,128]{1,0:T(8,128)S(1)} copy-done((f32[16,128]{1,0:T(8,128)S(1)}, f32[16,128]{1,0:T(8,128)}, u32[]{:S(2)}) %copy-start.3) | copy-done | bytes 8216
  4.5 56.1 %shard_map.76 = (f32[16,64,128]{2,1,0:T(8,128)S(1)}, f32[16,64]{1,0:T(8,128)S(1)}, f32[16,64]{1,0:T(8,128)S(1)}) custom-call(f32[16,64,128]{2,1,0:T(8,128)S(1)} %bitcast.3, f32[8,8,128]{2,1,0:T(8,128)S(1)} %copy-done.1, s32[16,128]{1,0:T(8,128)S(1)} %copy-done.2, f32[16,128]{1,0:T(8,128)S(1)} %copy-done.3, f32[1,16]{1,0:T(1,128)S(1)} %bitcast.5), custom_call_target="tpu_custom_call" | custom-call | tf_op jit(solution)/shard_map/pallas_call | solution.py:429
  60.6 0.8 %copy.11 = f32[16,8,8,128]{3,2,1,0:T(8,128)} copy(f32[16,8,8,128]{3,2,1,0:T(8,128)S(1)} %bitcast.4) | data formatting | bytes 1048576
  61.4 0.6 copy.12
  62.0 0.6 copy.13
Async XLA Ops:
  0.6 0.7 %copy-start.4 = (f32[16]{0:T(128)S(1)}, f32[16]{0:T(128)}, u32[]{:S(2)}) copy-start(f32[16]{0:T(128)} %param.9) | copy-start | bytes 196
  1.3 1.0 %copy-start = (f32[16,8,8,128]{3,2,1,0:T(8,128)S(1)}, f32[16,8,8,128]{3,2,1,0:T(8,128)}, u32[]{:S(2)}) copy-start(f32[16,8,8,128]{3,2,1,0:T(8,128)} %param.5) | copy-start | bytes 1572868
  2.3 0.8 %copy-start.1 = (f32[8,8,128]{2,1,0:T(8,128)S(1)}, f32[8,8,128]{2,1,0:T(8,128)}, u32[]{:S(2)}) copy-start(f32[8,8,128]{2,1,0:T(8,128)} %potential.1) | copy-start | bytes 98308
  3.1 0.7 %copy-start.2 = (s32[16,128]{1,0:T(8,128)S(1)}, s32[16,128]{1,0:T(8,128)}, u32[]{:S(2)}) copy-start(s32[16,128]{1,0:T(8,128)} %index_ref.1) | copy-start | bytes 24580
  3.8 0.7 %copy-start.3 = (f32[16,128]{1,0:T(8,128)S(1)}, f32[16,128]{1,0:T(8,128)}, u32[]{:S(2)}) copy-start(f32[16,128]{1,0:T(8,128)} %value_ref.1) | copy-start | bytes 24580
